TPU v7x, 32 devices: a whole 2x2x4 slice. The times are simulated.
32 devices in a mesh: dp: 4 (over x, core), mp: 8 (over z, y).
Axes of the slice: x: 2, y: 2, z: 4, core: 2. Of those that a mesh axis runs over, the one named last changes fastest.
Arguments:
- tokens: bfloat16 [32768, 768], P(('dp', 'mp')), may hold values from -6 to 6
- lengths: int32 [64], P(('dp', 'mp')), may hold values from 16 to 512, as said below
- w_in: bfloat16 [768, 3072], P('dp', 'mp'), may hold values from -0.21875 to 0.21875
- b_in: bfloat16 [3072], P('mp'), may hold values from -3 to 3
- w_out: bfloat16 [3072, 768], P('mp', 'dp'), may hold values from -0.109375 to 0.109375
- b_out: float32 [768], replicated, may hold values from -2 to 2
- gain_mix: float32 [768], replicated, may hold values from 0.25 to 1.75
- shift_mix: float32 [768], replicated, may hold values from -2 to 2
- gain_ffn: float32 [768], replicated, may hold values from 0.25 to 1.75
- shift_ffn: float32 [768], replicated, may hold values from -2 to 2
- cotangent: bfloat16 [32768, 768], P(('dp', 'mp')), may hold values from -6 to 6
Outputs:
- layer_out: bfloat16 [32768, 768], P(('dp', 'mp'))
- grad_tokens: bfloat16 [32768, 768], P(('dp', 'mp'))
- grad_w_in: float32 [768, 3072], P('dp', 'mp')
- grad_b_in: float32 [3072], replicated
- grad_w_out: float32 [3072, 768], P('mp', 'dp')
- grad_b_out: float32 [768], replicated
- grad_gain_mix: float32 [768], replicated
- grad_shift_mix: float32 [768], replicated
- grad_gain_ffn: float32 [768], replicated
- grad_shift_ffn: float32 [768], replicated
Inputs may be any that keep to these rules, and one draw needn't show every extreme that they name: `lengths`: in every aligned block of 8 items exactly one has length 512; the others have at most 256.
All inputs are finite; a program needn't handle non-finite values.
Results may differ from a plain program's by a relative error of at most 0.0095.
Values may be sent and summed in bfloat16 or wider, within the bound.
No kernel may reach another device: no remote copies, remote signals or barrier semaphores. Data moves between devices by JAX's collectives and lax.ppermute only.
A program may use at most 320 MiB of HBM per device.

v0:
```python
from functools import partial
import math

import jax
import jax.numpy as jnp
from jax import lax
from jax.sharding import PartitionSpec as P

D = 768
FF = 3072
LEN = 512
MB = 2
SEQ_MB = 1


epsilon = 1e-06


def dft_tables(width):
    index = jnp.arange(width, dtype=jnp.int32)
    phase = index[:, None] * index[None, :] % width
    angle = phase.astype(jnp.float32) * (2.0 * math.pi / width)
    factor = 1.0 / math.sqrt(width)
    return (jnp.cos(angle) * factor, jnp.sin(angle) * factor)


def layer_norm(values, gain, shift):
    center = values - jnp.mean(values, axis=-1, keepdims=True)
    spread = jnp.mean(center * center, axis=-1, keepdims=True)
    return center * lax.rsqrt(spread + epsilon) * gain + shift


def masked_norm(values, gain, shift, live_mask):
    return live_mask * layer_norm(values, gain, shift)


def inner_rows(left, right):
    return lax.dot_general(
        left, right, (((1,), (1,)), ((), ())), preferred_element_type=jnp.float32
    )


def outer_rows(left, right):
    return lax.dot_general(
        left, right, (((0,), (0,)), ((), ())), preferred_element_type=jnp.float32
    )


def body(
    tokens, lengths, w_in, b_in, w_out, b_out, gain_mix, shift_mix, gain_ffn, shift_ffn, cotangent
):
    ff_local = w_in.shape[1]
    tok_rows = SEQ_MB * LEN
    cos_feat, sin_feat = dft_tables(D)
    feat_table = jnp.concatenate([cos_feat, sin_feat], axis=1).astype(jnp.bfloat16)
    cos_seq, sin_seq = dft_tables(LEN)
    seq_table = jnp.concatenate([cos_seq, -sin_seq], axis=1).astype(jnp.bfloat16)
    w_out_turned = w_out.T
    grad_w_in = jnp.zeros((D, ff_local), jnp.float32)
    grad_w_turned = jnp.zeros((D, ff_local), jnp.float32)
    grad_b_in = jnp.zeros((ff_local,), jnp.float32)
    grad_b_out = jnp.zeros((D,), jnp.float32)
    grad_gain_mix = jnp.zeros((D,), jnp.float32)
    grad_shift_mix = jnp.zeros((D,), jnp.float32)
    grad_gain_ffn = jnp.zeros((D,), jnp.float32)
    grad_shift_ffn = jnp.zeros((D,), jnp.float32)
    positions = jnp.arange(LEN, dtype=jnp.int32)
    outputs = []
    input_grads = []
    for micro in range(MB):
        inputs = lax.slice_in_dim(tokens, micro * tok_rows, (micro + 1) * tok_rows, axis=0)
        cot_part = lax.slice_in_dim(cotangent, micro * tok_rows, (micro + 1) * tok_rows, axis=0)
        item_lengths = lax.slice_in_dim(lengths, micro * SEQ_MB, (micro + 1) * SEQ_MB, axis=0)
        live_mask = (
            (positions[None, :] < item_lengths[:, None]).astype(jnp.float32).reshape(tok_rows, 1)
        )
        masked = inputs * live_mask.astype(jnp.bfloat16)
        spectra = jnp.dot(masked, feat_table, preferred_element_type=jnp.float32).astype(
            jnp.bfloat16
        )
        stacked = (
            spectra.reshape(SEQ_MB, LEN, 2, D).transpose(0, 2, 1, 3).reshape(SEQ_MB, 2 * LEN, D)
        )
        mixed = jnp.einsum(
            "st,gtd->gsd", seq_table, stacked, preferred_element_type=jnp.float32
        ).reshape(tok_rows, D)
        first, first_back = jax.vjp(
            layer_norm, masked.astype(jnp.float32) + mixed, gain_mix, shift_mix
        )
        first_low = first.astype(jnp.bfloat16)
        w_in_rows, w_out_rows = (
            lax.all_gather(w_in, "dp", axis=0, tiled=True),
            lax.all_gather(w_out_turned, "dp", axis=0, tiled=True),
        )
        gathered = lax.all_gather(first_low, "mp", axis=0, tiled=True)
        pre_act = jnp.dot(gathered, w_in_rows, preferred_element_type=jnp.float32) + b_in.astype(
            jnp.float32
        )
        activation, gelu_back = jax.vjp(jax.nn.gelu, pre_act)
        hidden = activation.astype(jnp.bfloat16)
        branch = (
            lax.psum_scatter(inner_rows(hidden, w_out_rows), "mp", scatter_dimension=0, tiled=True)
            + b_out
        )
        result, last_back = jax.vjp(
            partial(masked_norm, live_mask=live_mask), first + branch, gain_ffn, shift_ffn
        )
        outputs.append(result.astype(jnp.bfloat16))
        grad_second, gain_part, shift_part = last_back(cot_part.astype(jnp.float32))
        grad_gain_ffn = grad_gain_ffn + gain_part
        grad_shift_ffn = grad_shift_ffn + shift_part
        grad_branch = grad_second.astype(jnp.bfloat16)
        grad_b_out = grad_b_out + jnp.sum(grad_branch.astype(jnp.float32), axis=0)
        grad_gathered = lax.all_gather(grad_branch, "mp", axis=0, tiled=True)
        grad_hidden = jnp.dot(grad_gathered, w_out_rows, preferred_element_type=jnp.float32)
        grad_pre = gelu_back(grad_hidden)[0].astype(jnp.bfloat16)
        grad_b_in = grad_b_in + jnp.sum(grad_pre.astype(jnp.float32), axis=0)
        grad_w_in = grad_w_in + outer_rows(gathered, grad_pre)
        grad_w_turned = grad_w_turned + outer_rows(grad_gathered, hidden)
        grad_ffn = lax.psum_scatter(
            inner_rows(grad_pre, w_in_rows), "mp", scatter_dimension=0, tiled=True
        )
        grad_sum, gain_part, shift_part = first_back(grad_second + grad_ffn)
        grad_gain_mix = grad_gain_mix + gain_part
        grad_shift_mix = grad_shift_mix + shift_part
        grad_mixed = grad_sum.astype(jnp.bfloat16).reshape(SEQ_MB, LEN, D)
        grad_stack = jnp.einsum(
            "st,gsd->gtd", seq_table, grad_mixed, preferred_element_type=jnp.float32
        ).astype(jnp.bfloat16)
        grad_spectra = (
            grad_stack.reshape(SEQ_MB, 2, LEN, D).transpose(0, 2, 1, 3).reshape(tok_rows, 2 * D)
        )
        grad_masked = grad_sum + inner_rows(grad_spectra, feat_table)
        input_grads.append((grad_masked * live_mask).astype(jnp.bfloat16))
    offset = lax.axis_index("mp") * ff_local
    bias_grad_full = lax.dynamic_update_slice(jnp.zeros((FF,), jnp.float32), grad_b_in, (offset,))
    grad_w_in_part, grad_w_turned_part = (
        lax.psum_scatter(
            grad_w_in.astype(jnp.bfloat16), "dp", scatter_dimension=0, tiled=True
        ).astype(jnp.float32),
        lax.psum_scatter(
            grad_w_turned.astype(jnp.bfloat16), "dp", scatter_dimension=0, tiled=True
        ).astype(jnp.float32),
    )
    summed = lax.psum(
        (bias_grad_full, grad_b_out, grad_gain_mix, grad_shift_mix, grad_gain_ffn, grad_shift_ffn),
        ("dp", "mp"),
    )
    return (
        jnp.concatenate(outputs, axis=0),
        jnp.concatenate(input_grads, axis=0),
        grad_w_in_part,
        summed[0],
        grad_w_turned_part.T,
        summed[1],
        summed[2],
        summed[3],
        summed[4],
        summed[5],
    )


def solution(mesh):
    return jax.shard_map(
        body,
        mesh=mesh,
        in_specs=(
            P(("dp", "mp"), None),
            P(("dp", "mp")),
            P("dp", "mp"),
            P("mp"),
            P("mp", "dp"),
            P(),
            P(),
            P(),
            P(),
            P(),
            P(("dp", "mp"), None),
        ),
        out_specs=(
            P(("dp", "mp"), None),
            P(("dp", "mp"), None),
            P("dp", "mp"),
            P(),
            P("mp", "dp"),
            P(),
            P(),
            P(),
            P(),
            P(),
        ),
        check_vma=False,
    )
```

profile of v0, /device:TPU:0, one launch (start us, length us, event | category | flops | bytes accessed | tf_op | source)
XLA Modules:
  0.0 1429.9 jit_solution(16443774621906451339)
XLA Ops:
  7.2 5.4 negate_convert_fusion
  12.6 10.7 multiply_convert_fusion.2
  23.3 0.6 fusion.60
  23.9 0.6 fusion.46
  24.6 0.7 fusion.45
  25.4 1.2 copy.55
  26.8 0.9 copy-done.17
  27.7 3.0 convolution_convert_fusion
  31.4 0.9 copy-done.18
  32.6 1.0 fusion.61
  34.1 0.9 copy-done.11
  35.0 2.6 convolution_convert_fusion.1
  37.6 3.6 reshape.228
  41.5 0.9 copy-done.16
  42.7 1.0 fusion.62
  44.4 1.6 fusion.25
  46.1 0.7 all-gather.7.cloned.1.call-update
  47.0 9.4 all_gather.21
  56.4 8.5 all_gather.22
  65.0 83.5 %all-gather.5.cloned.1.call-done = bf16[4096,768]{0,1:T(8,128)(2,1)} async-done(((bf16[512,768]{0,1:T(8,128)(2,1)}), bf16[4096,768]{0,1:T(8,128)(2,1)}) %all-gather.5.cloned.1.call-update) | async-done | bytes 6291472 | tf_op jit(solution)/shard_map/all_gather | solution.py:95
  148.5 5.9 convolution_add_fusion.1
  154.3 2.7 copy-done.36
  157.1 6.6 fusion.51
  163.7 85.1 %all-gather.7.cloned.1.call-done = bf16[4096,768]{0,1:T(8,128)(2,1)} async-done(((bf16[512,768]{0,1:T(8,128)(2,1)}), bf16[4096,768]{0,1:T(8,128)(2,1)}) %all-gather.7.cloned.1.call-update) | async-done | bytes 6291472 | tf_op jit(solution)/shard_map/all_gather | solution.py:95
  248.8 5.9 convolution_add_fusion
  254.7 2.6 copy-done.37
  257.3 6.5 fusion.49
  263.8 2.6 fusion.58
  266.4 2.3 copy.58
  268.8 2.3 copy.57
  271.1 1.3 fusion.39
  272.4 186.1 %reduce-scatter.7.cloned.1.call-done = f32[512,768]{0,1:T(8,128)} async-done(((f32[4096,768]{0,1:T(8,128)}), f32[512,768]{0,1:T(8,128)}) %reduce-scatter.7.cloned.1.call-update) | async-done | bytes 1572880 | tf_op jit(solution)/shard_map/reduce_scatter | solution.py:102
  458.4 210.4 %reduce-scatter.9.cloned.1.call-done = f32[512,768]{0,1:T(8,128)} async-done(((f32[4096,768]{0,1:T(8,128)}), f32[512,768]{0,1:T(8,128)}) %reduce-scatter.9.cloned.1.call-update) | async-done | bytes 1572880 | tf_op jit(solution)/shard_map/reduce_scatter | solution.py:102
  668.9 2.8 fusion.57
  671.8 1.1 multiply_reduce_fusion.7
  672.9 0.8 multiply_reduce_fusion.1
  673.7 1.5 convert_reduce_fusion.3
  675.3 3.2 convert_reduce_fusion.2
  678.7 95.3 %all-gather.9.cloned.1.call-done = bf16[4096,768]{0,1:T(8,128)(2,1)} async-done(((bf16[512,768]{0,1:T(8,128)(2,1)}), bf16[4096,768]{0,1:T(8,128)(2,1)}) %all-gather.9.cloned.1.call-update) | async-done | bytes 6291472 | tf_op jit(solution)/shard_map/all_gather | solution.py:114
  774.0 11.4 convert_reduce_fusion.1
  785.4 88.2 %all-gather.11.cloned.1.call-done = bf16[4096,768]{0,1:T(8,128)(2,1)} async-done(((bf16[512,768]{0,1:T(8,128)(2,1)}), bf16[4096,768]{0,1:T(8,128)(2,1)}) %all-gather.11.cloned.1.call-update) | async-done | bytes 6291472 | tf_op jit(solution)/shard_map/all_gather | solution.py:114
  873.6 10.4 convert_reduce_fusion
  884.0 6.7 fusion.65
  890.7 6.5 fusion.23
  897.5 8.2 fusion.50
  905.7 9.0 fusion.24
  914.7 10.0 fusion.64
  925.1 10.1 fusion.63
  935.4 1.7 convert_element_type.192
  937.0 5.2 reduce-scatter.17.cloned.1.call-done
  942.2 1.6 convert_bitcast_fusion
  943.8 209.8 %reduce-scatter.13.cloned.1.call-done = f32[512,768]{0,1:T(8,128)} async-done(((f32[4096,768]{0,1:T(8,128)}), f32[512,768]{0,1:T(8,128)}) %reduce-scatter.13.cloned.1.call-update) | async-done | bytes 1572880 | tf_op jit(solution)/shard_map/reduce_scatter | solution.py:120
  1153.7 4.0 multiply_reduce_fusion.2
  1157.7 206.4 %reduce-scatter.11.cloned.1.call-done = f32[512,768]{0,1:T(8,128)} async-done(((f32[4096,768]{0,1:T(8,128)}), f32[512,768]{0,1:T(8,128)}) %reduce-scatter.11.cloned.1.call-update) | async-done | bytes 1572880 | tf_op jit(solution)/shard_map/reduce_scatter | solution.py:120
  1364.1 3.3 multiply_reduce_fusion.3
  1367.4 2.6 fusion.54
  1370.2 1.6 copy.47
  1371.8 2.7 convolution_convert_fusion.2
  1374.7 1.3 copy-done.10
  1376.3 1.4 multiply_convert_fusion.4
  1377.9 1.0 convolution_convert_fusion.3
  1379.0 1.4 multiply_convert_fusion.5
  1380.7 1.6 copy.48
  1382.2 40.4 %all-reduce = (f32[3072]{0:T(1024)}, f32[768]{0:T(1024)}, f32[768]{0:T(1024)}, f32[768]{0:T(1024)}, f32[768]{0:T(1024)}, /*index=5*/f32[768]{0:T(1024)}) all-reduce(f32[3072]{0:T(1024)S(1)} %add_dynamic-update-slice_fusion, f32[768]{0:T(1024)S(1)} %add.235, f32[768]{0:T(1024)S(1)} %add.236, ...), channel_id=1, replica_groups=mesh['dp'=4,'mp'=8] {'dp','mp'}, use_global_device_ids=true, to_apply=%region_23.24 | all-reduce | flops 6912 | bytes 55296 | tf_op jit(solution)/shard_map/psum | solution.py:145
  (122 shorter events, 5.7 us)
Async XLA Ops:
  7.2 16.2 %copy-start.34 = (s32[2]{0:T(128)S(1)}, s32[2]{0:T(128)}, u32[]{:S(2)}) copy-start(s32[2]{0:T(128)} %param.12) | copy-start | bytes 28
  7.2 18.1 %copy-start.8 = (bf16[1024,768]{1,0:T(8,128)(2,1)S(1)}, bf16[1024,768]{1,0:T(8,128)(2,1)}, u32[]{:S(2)}) copy-start(bf16[1024,768]{1,0:T(8,128)(2,1)} %param.11) | copy-start | bytes 4718596
  7.2 141.3 %all-gather.5.cloned.1.call-start = ((), (), s32[]{:S(2)}) async-start(), calls=%async_computation.6 | async-start | bytes 7077888 | tf_op jit(solution)/shard_map/all_gather | solution.py:95
  26.8 0.9 copy-start.17
  31.1 1.1 copy-start.18
  31.2 1.3 copy-start.21
  31.2 1.4 copy-start.24
  32.6 1.3 copy-start.13
  32.6 1.5 copy-start.15
  33.6 1.4 copy-start.11
  41.2 1.1 copy-start.16
  41.2 1.3 copy-start.22
  41.3 1.4 copy-start.25
  43.7 0.7 copy-start.30
  43.7 0.7 copy-start.32
  46.1 0.8 copy-start.35
  46.1 0.9 copy-start.28
  46.1 10.4 copy-start.29
  46.1 202.7 %all-gather.7.cloned.1.call-start = ((), (), s32[]{:S(2)}) async-start(), calls=%async_computation.8 | async-start | bytes 7077888 | tf_op jit(solution)/shard_map/all_gather | solution.py:95
  46.9 411.6 %reduce-scatter.7.cloned.1.call-start = ((), (), s32[]{:S(2)}) async-start(), calls=%async_computation.7 | async-start | bytes 14155776 | tf_op jit(solution)/shard_map/reduce_scatter | solution.py:102
  148.5 8.6 copy-start.19
  154.3 2.7 copy-start.36
  163.7 505.2 %reduce-scatter.9.cloned.1.call-start = ((), (), s32[]{:S(2)}) async-start(), calls=%async_computation.9 | async-start | bytes 14155776 | tf_op jit(solution)/shard_map/reduce_scatter | solution.py:102
  248.8 8.5 copy-start.20
  254.6 2.6 copy-start.37
  263.8 510.3 %all-gather.9.cloned.1.call-start = ((), (), s32[]{:S(2)}) async-start(), calls=%async_computation.10 | async-start | bytes 7077888 | tf_op jit(solution)/shard_map/all_gather | solution.py:114
  266.4 402.5 %copy-start.33 = (f32[768]{0:T(1024)S(1)}, f32[768]{0:T(1024)}, u32[]{:S(2)}) copy-start(f32[768]{0:T(1024)} %param.16) | copy-start | bytes 9220
  272.4 399.4 %copy-start.27 = (f32[768]{0:T(1024)S(1)}, f32[768]{0:T(1024)}, u32[]{:S(2)}) copy-start(f32[768]{0:T(1024)} %param.19) | copy-start | bytes 9220
  668.9 2.9 copy-start.2
  668.9 2.9 copy-start.3
  671.7 2.0 copy-start
  671.7 2.0 copy-start.1
  675.3 198.3 %all-gather.11.cloned.1.call-start = ((), (), s32[]{:S(2)}) async-start(), calls=%async_computation.12 | async-start | bytes 7077888 | tf_op jit(solution)/shard_map/all_gather | solution.py:114
  678.5 256.9 %reduce-scatter.15.cloned.1.call-start = ((), (), s32[]{:S(2)}) async-start(), calls=%async_computation.14 | async-start | bytes 737280 | tf_op jit(solution)/shard_map/reduce_scatter | solution.py:138
  873.6 10.4 copy-start.5
  884.0 6.7 copy-start.6
  897.2 45.0 %reduce-scatter.17.cloned.1.call-start = ((), (), s32[]{:S(2)}) async-start(), calls=%async_computation.15 | async-start | bytes 737280 | tf_op jit(solution)/shard_map/reduce_scatter | solution.py:141
  914.7 239.0 %reduce-scatter.13.cloned.1.call-start = ((), (), s32[]{:S(2)}) async-start(), calls=%async_computation.13 | async-start | bytes 14155776 | tf_op jit(solution)/shard_map/reduce_scatter | solution.py:120
  924.8 439.3 %reduce-scatter.11.cloned.1.call-start = ((), (), s32[]{:S(2)}) async-start(), calls=%async_computation.11 | async-start | bytes 14155776 | tf_op jit(solution)/shard_map/reduce_scatter | solution.py:120
  935.2 218.5 %copy-start.31 = (f32[768]{0:T(1024)S(1)}, f32[768]{0:T(1024)}, u32[]{:S(2)}) copy-start(f32[768]{0:T(1024)} %param.20) | copy-start | bytes 9220
  1364.1 3.3 copy-start.4
  1367.4 2.6 copy-start.7
  1371.8 2.9 copy-start.14
  1374.5 1.4 copy-start.10
  1374.5 1.7 copy-start.12
  1376.3 1.4 copy-start.9
  1376.3 1.5 copy-start.23
  1376.3 1.7 copy-start.26
Sparse Core Ops, SparseCore 0:
  46.2 102.1 all-gather.4
  151.1 97.6 all-gather.6
  252.4 206.0 reduce-scatter.6
  461.9 206.9 reduce-scatter.8
  675.4 98.5 all-gather.8
  775.9 97.6 all-gather.10
  897.3 20.2 reduce-scatter.14
  920.1 22.0 reduce-scatter.16
  945.8 207.8 reduce-scatter.12
  1157.1 206.9 reduce-scatter.10
where the time goes:
time: 1440 us; the launch traced here: 1430 us
  waiting for transfers between devices  1170 us (81%)
  matrix products  111 us (8%)
  blocking collectives  58.3 us (4%)
  other arithmetic  44 us (3%)
  local copies, waits for them, and re-layouts  29.4 us (2%)
  between operations  15.2 us (1%)
    reduce_scatter x2, waiting for transfers between devices, body(): lax.psum_scatter(inner_rows(grad_pre, w_in_rows), 'mp', scatter_dimension...  416 us
    reduce_scatter x2, waiting for transfers between devices, body(): lax.psum_scatter(inner_rows(hidden, w_out_rows), 'mp', scatter_dimension=...  397 us
    all_gather x2, waiting for transfers between devices, body(): grad_gathered = lax.all_gather(grad_branch, 'mp', axis=0, tiled=True)  184 us
    all_gather x2, waiting for transfers between devices, body(): gathered = lax.all_gather(first_low, 'mp', axis=0, tiled=True)  169 us
    psum x1, blocking collectives, body(): lax.psum((bias_grad_full, grad_b_out, grad_gain_mix, grad_shift_mix, grad...  40.4 us
    dot_general x6, matrix products, inner_rows(): lax.dot_general(left, right, (((1,), (1,)), ((), ())), preferred_element_...  35.9 us
    dot_general x4, matrix products, outer_rows(): lax.dot_general(left, right, (((0,), (0,)), ((), ())), preferred_element_...  30.3 us
  transfers between devices with their start and end apart: 10, of which 9 were waited for; matrix products, arithmetic and copies ran while one was open for 6% of the time, Pallas kernels for 0%

commit v1 on v0

v1 whole, which is shorter than its diff:
```python
from functools import partial
import math

import jax
import jax.numpy as jnp
from jax import lax
from jax.experimental import pallas as pl
from jax.experimental.pallas import tpu as pltpu
from jax.sharding import PartitionSpec as P

D = 768
FF = 3072
LEN = 512
HALF = LEN // 2
ROWS = LEN + HALF

epsilon = 1e-06
GELU_C = math.sqrt(2.0 / math.pi)


def dft_tables(width):
    index = jnp.arange(width, dtype=jnp.int32)
    phase = index[:, None] * index[None, :] % width
    angle = phase.astype(jnp.float32) * (2.0 * math.pi / width)
    factor = 1.0 / math.sqrt(width)
    return (jnp.cos(angle) * factor, jnp.sin(angle) * factor)


def layer_norm(values, gain, shift):
    center = values - jnp.mean(values, axis=-1, keepdims=True)
    spread = jnp.mean(center * center, axis=-1, keepdims=True)
    return center * lax.rsqrt(spread + epsilon) * gain + shift


def masked_norm(values, gain, shift, live_mask):
    return live_mask * layer_norm(values, gain, shift)


def inner_rows(left, right):
    return lax.dot_general(
        left, right, (((1,), (1,)), ((), ())), preferred_element_type=jnp.float32
    )


def dot(left, right):
    return jnp.dot(left, right, preferred_element_type=jnp.float32)


def forward_kernel(first_ref, weights_ref, bias_ref, pre_ref, branch_ref):
    width = pre_ref.shape[-1]
    chunk = pl.program_id(0)

    @pl.when(chunk == 0)
    def _():
        branch_ref[...] = jnp.zeros_like(branch_ref)

    pre = dot(first_ref[...], weights_ref[0, :, :width]) + bias_ref[0]
    pre_ref[0] = pre
    inner = jnp.tanh(GELU_C * (pre + 0.044715 * (pre * pre * pre)))
    hidden = (0.5 * pre * (1.0 + inner)).astype(jnp.bfloat16)
    branch_ref[...] += inner_rows(hidden, weights_ref[0, :, width:])


def backward_kernel(
    grad_ref, grad_turned_ref, first_turned_ref, weights_ref, pre_ref, grad_w_ref, bias_ref, ffn_ref
):
    width = pre_ref.shape[-1]
    chunk = pl.program_id(0)

    @pl.when(chunk == 0)
    def _():
        ffn_ref[...] = jnp.zeros_like(ffn_ref)

    grad_hidden = dot(grad_ref[...], weights_ref[0, :, width:])
    pre = pre_ref[0]
    square = pre * pre
    inner = jnp.tanh(GELU_C * (pre + 0.044715 * (square * pre)))
    outer = 0.5 * (1.0 + inner)
    hidden = (pre * outer).astype(jnp.bfloat16)
    slope = outer + (0.5 * GELU_C) * pre * (1.0 - inner * inner) * (1.0 + (3 * 0.044715) * square)
    grad_pre = (grad_hidden * slope).astype(jnp.bfloat16)
    bias_ref[0] = jnp.sum(grad_pre.astype(jnp.float32), axis=0, keepdims=True)
    grad_w_ref[0, :, width:] = dot(grad_turned_ref[...], hidden).astype(jnp.bfloat16)
    grad_w_ref[0, :, :width] = dot(first_turned_ref[...], grad_pre).astype(jnp.bfloat16)
    ffn_ref[...] += inner_rows(grad_pre, weights_ref[0, :, :width])


def whole(shape):
    return pl.BlockSpec(shape, lambda m: (0,) * len(shape))


def chunked(shape):
    return pl.BlockSpec((1,) + shape, lambda m: (m,) + (0,) * len(shape))


def feed_forward(first_low, weights, bias):
    chunks, _, both = weights.shape
    width = both // 2
    rows = first_low.shape[0]
    return pl.pallas_call(
        forward_kernel,
        grid=(chunks,),
        in_specs=[whole((rows, D)), chunked((D, both)), chunked((1, width))],
        out_specs=[chunked((rows, width)), whole((rows, D))],
        out_shape=[
            jax.ShapeDtypeStruct((chunks, rows, width), jnp.float32),
            jax.ShapeDtypeStruct((rows, D), jnp.float32),
        ],
        cost_estimate=pl.CostEstimate(
            flops=4 * rows * D * width * chunks,
            bytes_accessed=chunks * (2 * D * both + 4 * rows * width) + 6 * rows * D,
            transcendentals=rows * width * chunks,
        ),
        name="ffn_forward",
    )(first_low, weights, bias)


def feed_backward(grad_branch, first_low, weights, pre):
    chunks, rows, width = pre.shape
    both = 2 * width
    return pl.pallas_call(
        backward_kernel,
        grid=(chunks,),
        in_specs=[
            whole((rows, D)),
            whole((D, rows)),
            whole((D, rows)),
            chunked((D, both)),
            chunked((rows, width)),
        ],
        out_specs=[chunked((D, both)), chunked((1, width)), whole((rows, D))],
        out_shape=[
            jax.ShapeDtypeStruct((chunks, D, both), jnp.bfloat16),
            jax.ShapeDtypeStruct((chunks, 1, width), jnp.float32),
            jax.ShapeDtypeStruct((rows, D), jnp.float32),
        ],
        cost_estimate=pl.CostEstimate(
            flops=8 * rows * D * width * chunks,
            bytes_accessed=chunks * (4 * D * both + 4 * rows * width) + 10 * rows * D,
            transcendentals=rows * width * chunks,
        ),
        name="ffn_backward",
    )(grad_branch, grad_branch.T, first_low.T, weights, pre)


def flips(size):
    bit = 1
    while bit < size:
        yield bit, [(i, i ^ bit) for i in range(size)]
        bit *= 2


def body(
    sizes,
    tokens, lengths, w_in, b_in, w_out, b_out, gain_mix, shift_mix, gain_ffn, shift_ffn, cotangent,
):
    width = w_in.shape[1]
    parts = sizes["mp"]
    shard = jnp.concatenate([w_in, w_out.T], axis=1)
    weights = lax.all_gather(shard, ("mp", "dp"), axis=0, tiled=True).reshape(parts, D, 2 * width)
    held = b_in.astype(jnp.bfloat16)[None]
    for _, pairs in flips(parts):
        held = jnp.concatenate([held, lax.ppermute(held, "mp", pairs)], axis=0)
    order = jnp.arange(parts, dtype=jnp.int32) ^ lax.axis_index("mp")
    bias = held[order].astype(jnp.float32)[:, None, :]

    long = jnp.where(lengths[0] > HALF, 0, 1)
    lens = (lengths[long], lengths[1 - long])
    starts = (long * LEN, (1 - long) * LEN)

    def take(values):
        return jnp.concatenate(
            [
                lax.dynamic_slice_in_dim(values, starts[0], LEN, axis=0),
                lax.dynamic_slice_in_dim(values, starts[1], HALF, axis=0),
            ],
            axis=0,
        )

    def put(values):
        head, tail = values[:LEN], values[LEN:]
        rest = jnp.zeros((HALF, D), values.dtype)
        return jnp.where(
            long == 0,
            jnp.concatenate([head, tail, rest], axis=0),
            jnp.concatenate([tail, rest, head], axis=0),
        )

    spots = jnp.concatenate([jnp.arange(LEN, dtype=jnp.int32), jnp.arange(HALF, dtype=jnp.int32)])
    limits = jnp.where(jnp.arange(ROWS) < LEN, lens[0], lens[1])
    live_mask = (spots < limits).astype(jnp.float32)[:, None]

    cos_feat, sin_feat = dft_tables(D)
    feat_table = jnp.concatenate([cos_feat, sin_feat], axis=1).astype(jnp.bfloat16)
    cos_seq, sin_seq = dft_tables(LEN)
    cos_low, sin_low = cos_seq.astype(jnp.bfloat16), (-sin_seq).astype(jnp.bfloat16)
    seq_long = jnp.concatenate([cos_low, sin_low], axis=1)
    seq_short = jnp.concatenate([cos_low[:HALF, :HALF], sin_low[:HALF, :HALF]], axis=1)

    masked = take(tokens) * live_mask.astype(jnp.bfloat16)
    spectra = dot(masked, feat_table).astype(jnp.bfloat16)

    def stack(values):
        return jnp.concatenate([values[:, :D], values[:, D:]], axis=0)

    mixed = jnp.concatenate(
        [dot(seq_long, stack(spectra[:LEN])), dot(seq_short, stack(spectra[LEN:]))], axis=0
    )
    first, first_back = jax.vjp(layer_norm, masked.astype(jnp.float32) + mixed, gain_mix, shift_mix)
    first_low = first.astype(jnp.bfloat16)
    pre, branch = feed_forward(first_low, weights, bias)
    result, last_back = jax.vjp(
        partial(masked_norm, live_mask=live_mask), first + (branch + b_out), gain_ffn, shift_ffn
    )
    layer_out = put(result.astype(jnp.bfloat16))
    grad_second, grad_gain_ffn, grad_shift_ffn = last_back(take(cotangent).astype(jnp.float32))
    grad_branch = grad_second.astype(jnp.bfloat16)
    grad_b_out = jnp.sum(grad_branch.astype(jnp.float32), axis=0)
    grad_w, grad_bias, grad_ffn = feed_backward(grad_branch, first_low, weights, pre)
    grad_shard = lax.psum_scatter(
        grad_w.reshape(parts * D, 2 * width), ("mp", "dp"), scatter_dimension=0, tiled=True
    ).astype(jnp.float32)
    grad_sum, grad_gain_mix, grad_shift_mix = first_back(grad_second + grad_ffn)
    grad_mixed = grad_sum.astype(jnp.bfloat16)

    def back(table, values):
        turned = lax.dot_general(
            table, values, (((0,), (0,)), ((), ())), preferred_element_type=jnp.float32
        ).astype(jnp.bfloat16)
        count = values.shape[0]
        return jnp.concatenate([turned[:count], turned[count:]], axis=1)

    grad_spectra = jnp.concatenate(
        [back(seq_long, grad_mixed[:LEN]), back(seq_short, grad_mixed[LEN:])], axis=0
    )
    grad_masked = grad_sum + inner_rows(grad_spectra, feat_table)
    grad_tokens = put((grad_masked * live_mask).astype(jnp.bfloat16))

    totals = jnp.concatenate(
        [grad_bias.reshape(-1), grad_b_out, grad_gain_mix, grad_shift_mix, grad_gain_ffn, grad_shift_ffn]
    )
    for axis in ("dp", "mp"):
        for _, pairs in flips(sizes[axis]):
            totals = totals + lax.ppermute(totals, axis, pairs)
    sums = [totals[FF + i * D : FF + (i + 1) * D] for i in range(5)]
    return (
        layer_out,
        grad_tokens,
        grad_shard[:, :width],
        totals[:FF],
        grad_shard[:, width:].T,
        *sums,
    )


def solution(mesh):
    rows = P(("dp", "mp"), None)
    return jax.shard_map(
        partial(body, dict(mesh.shape)),
        mesh=mesh,
        in_specs=(
            rows, P(("dp", "mp")), P("dp", "mp"), P("mp"), P("mp", "dp"),
            P(), P(), P(), P(), P(), rows,
        ),
        out_specs=(rows, rows, P("dp", "mp"), P(), P("mp", "dp"), P(), P(), P(), P(), P()),
        check_vma=False,
    )
```

time: 1440 us -> 296 us (0.21)
  waiting for transfers between devices: 1170 us -> 147 us
  matrix products: 111 us -> 6.85 us
  blocking collectives: 58.3 us -> 0 us
  Pallas kernels: 0 us -> 41.7 us
    reduce_scatter x6 -> x1, waiting for transfers between devices: 818 us -> 103 us  [body(): lax.psum_scatter(grad_w.reshape(parts * D, 2 * width), ('mp', 'dp'), scat...]
    all_gather x4 -> x1, waiting for transfers between devices: 352 us -> 37.1 us  [body(): lax.all_gather(shard, ('mp', 'dp'), axis=0, tiled=True)]
    dot_general x14 -> x5, matrix products: 75.2 us -> 4.86 us  [the longest x3 3.53 us: dot(): return jnp.dot(left, right, preferred_element_type=jnp.float32)]
    pallas_call x0 -> x2, Pallas kernels: none -> 41.7 us  [the longest x1 25.8 us: feed_backward(): pl.pallas_call(backward_kernel, grid=(chunks,), in_specs=[whole((rows, D)...]
    psum x1 -> x0, blocking collectives: 40.4 us -> none  [body(): lax.psum((bias_grad_full, grad_b_out, grad_gain_mix, grad_shift_mix, grad...]
    dot_general x6 -> x1, matrix products: 35.9 us -> 1.99 us  [inner_rows(): lax.dot_general(left, right, (((1,), (1,)), ((), ())), preferred_element_...]
    all_gather x2 -> x0, blocking collectives: 18 us -> none  [the longest x1 9.43 us: body(): lax.all_gather(w_in, 'dp', axis=0, tiled=True)]
  transfers between devices with their start and end apart: 10 -> 10, of which waited for: 9 -> 6; matrix products, arithmetic and copies ran while one was open for 6% -> 20% of each run, Pallas kernels for 0% -> 0%
where the time goes in v1:
time: 296 us; the launch traced here: 295 us
  waiting for transfers between devices  147 us (50%)
  Pallas kernels  41.7 us (14%)
  other arithmetic  38.3 us (13%)
  local copies, waits for them, and re-layouts  32.6 us (11%)
  between operations  15.3 us (5%)
  starting transfers between devices  13.8 us (5%)
  matrix products  6.85 us (2%)
    reduce_scatter x1, waiting for transfers between devices, body(): lax.psum_scatter(grad_w.reshape(parts * D, 2 * width), ('mp', 'dp'), scat...  103 us
    all_gather x1, waiting for transfers between devices, body(): lax.all_gather(shard, ('mp', 'dp'), axis=0, tiled=True)  37.1 us
    pallas_call x1, Pallas kernels, feed_backward(): pl.pallas_call(backward_kernel, grid=(chunks,), in_specs=[whole((rows, D)...  25.8 us
    pallas_call x1, Pallas kernels, feed_forward(): pl.pallas_call(forward_kernel, grid=(chunks,), in_specs=[whole((rows, D))...  15.8 us
    another operation x1, other arithmetic  10 us
    unnamed x71, local copies, waits for them, and re-layouts  9.3 us
    ppermute x3, starting transfers between devices, body(): held = jnp.concatenate([held, lax.ppermute(held, 'mp', pairs)], axis=0)  7.42 us
    reduce_sum x3, other arithmetic, layer_norm(): return center * lax.rsqrt(spread + epsilon) * gain + shift  7.22 us
  transfers between devices with their start and end apart: 10, of which 6 were waited for; matrix products, arithmetic and copies ran while one was open for 20% of the time, Pallas kernels for 0%

profile of v1, /device:TPU:0, one launch (start us, length us, event | category | flops | bytes accessed | tf_op | source)
XLA Modules:
  0.0 295.5 jit_solution(5455055044314215917)
XLA Ops:
  7.2 1.8 pad_maximum_fusion.7
  9.1 1.2 broadcast_in_dim.20
  10.4 3.0 %collective-permute-start = (bf16[1,384]{1,0:T(2,128)(2,1)}, bf16[1,384]{1,0:T(2,128)(2,1)}, u32[]{:S(2)}, u32[]{:S(2)}) collective-permute-start(bf16[1,384]{1,0:T(2,128)(2,1)} %broadcast_in_dim.20), channel_id=1, source_target_pairs={{0,1},{1,0},{2,3},{3,2},{4,5},{5,4},{6,7},{7,6},{8,9},{9,8},{10,11... | collective-permute-start | bytes 2312 | tf_op jit(solution)/shard_map/ppermute | solution.py:163
  14.0 1.9 constant_dynamic-slice_fusion
  16.2 2.1 constant_dynamic-slice_fusion.1
  18.6 4.4 %negate_convert_fusion = (bf16[512,512]{1,0:T(8,128)(2,1)S(1)}, bf16[512,512]{1,0:T(8,128)(2,1)S(1)}) fusion(), kind=kLoop, calls=%fused_computation.58 | loop fusion | flops 4980736 | bytes 1048576 | tf_op jit(solution)/shard_map/convert_element_type | solution.py:196
  23.1 0.7 fusion.55
  23.8 1.9 fusion.35
  25.7 10.0 %multiply_convert_fusion.2 = (bf16[768,768]{1,0:T(8,128)(2,1)S(1)}, bf16[768,768]{1,0:T(8,128)(2,1)S(1)}) fusion(), kind=kLoop, calls=%fused_computation.31 | loop fusion | flops 7667712 | bytes 2359296 | tf_op jit(solution)/shard_map/convert.2
  35.7 2.0 convolution_convert_fusion
  37.9 0.5 fusion.29
  38.5 1.0 fusion.18
  39.5 0.4 fusion.49
  40.3 0.6 copy-done.22
  40.8 1.4 fusion.56.first_turned_ref
  42.2 0.4 fusion.15
  42.6 0.7 pad_maximum_fusion.13
  43.3 1.6 collective-permute-start.1
  45.0 2.0 collective-permute-done.1
  47.0 0.7 pad_maximum_fusion.12
  47.7 2.8 collective-permute-start.2
  50.5 0.6 pad_clamp_fusion
  51.1 1.4 copy.25.first_ref
  52.5 1.2 copy.42
  53.7 1.4 copy.41
  55.1 0.7 pad_maximum_fusion.11
  55.8 1.3 gather_fusion
  57.1 1.3 reshape.152.bias_ref
  58.4 37.1 %all-gather.2.cloned.1.call-done = bf16[6144,768]{1,0:T(8,128)(2,1)} async-done(((bf16[192,768]{1,0:T(8,128)(2,1)}), bf16[6144,768]{1,0:T(8,128)(2,1)}) %all-gather.2.cloned.1.call-update) | async-done | bytes 9437200 | tf_op jit(solution)/shard_map/all_gather | solution.py:160
  95.6 15.8 %ffn_forward.1 = (f32[8,768,384]{2,1,0:T(8,128)}, f32[768,768]{1,0:T(8,128)}) custom-call(bf16[768,768]{1,0:T(8,128)(2,1)} %copy.25.first_ref, bf16[8,768,768]{2,1,0:T(8,128)(2,1)} %bitcast.20, f32[8,1,384]{2,1,0:T(1,128)} %reshape.152.bias_ref), custom_call_target="tpu_custom_call" | custom-call | flops 7247757312 | bytes 22413312 | tf_op jit(solution)/shard_map/ffn_forward/pallas_call | solution.py:100
  111.4 3.1 %copy.26 = f32[768,768]{0,1:T(8,128)} copy(f32[768,768]{1,0:T(8,128)} %get-tuple-element.15) | data formatting | bytes 4718592 | tf_op jit(solution)/shard_map/ffn_forward/pallas_call | solution.py:100
  114.5 2.3 fusion.48
  116.9 0.7 multiply_reduce_fusion.3
  117.6 1.9 multiply_reduce_fusion
  119.6 2.6 convert_reduce_fusion
  122.2 2.4 copy.29.grad_ref
  124.6 25.8 %ffn_backward.1 = (bf16[8,768,768]{2,1,0:T(8,128)(2,1)}, f32[8,1,384]{2,1,0:T(1,128)}, f32[768,768]{1,0:T(8,128)}) custom-call(bf16[768,768]{1,0:T(8,128)(2,1)} %copy.29.grad_ref, bf16[768,768]{1,0:T(8,128)(2,1)} %bitcast.16, bf16[768,768]{1,0:T(8,128)(2,1)} %fusion.56.first_turned_ref, bf16[8,768,768]{2,1,0:T(8,128)(2,1)} %bitcast.21, ...), custom_call_target="tpu_custom_call" | custom-call | flops 14495514624 | bytes 34209792 | tf_op jit(solution)/shard_map/ffn_backward/pallas_call | solution.py:121
  150.4 0.6 pad.12.clone
  151.0 3.1 %copy.30 = f32[768,768]{0,1:T(8,128)} copy(f32[768,768]{1,0:T(8,128)} %get-tuple-element.17) | data formatting | bytes 4718592 | tf_op jit(solution)/shard_map/ffn_backward/pallas_call | solution.py:121
  154.1 0.7 constant_dynamic-update-slice_fusion.5
  154.8 0.7 constant_dynamic-update-slice_fusion.4
  155.5 4.6 %multiply_reduce_fusion.1 = (f32[768]{0:T(1024)S(1)}, f32[768]{0:T(1024)S(1)}, f32[768]{0:T(1024)S(1)}, f32[768,768]{0,1:T(8,128)S(1)}, bf16[768,768]{0,1:T(8,128)(2,1)S(1)}) fusion(f32[768,768]{0,1:T(8,128)S(1)} %get-tuple-element.46, f32[768]{0:T(1024)S(1)} %fusion.36, f32[768]{0:T(1024)S(1)} %broadcast_multiply_fusion.1, f32[768]{0:T(1024)S(1)} %copy-done.15, ...), kind=kLoop, calls=%fused_computation.18 | loop fusion | flops 15333120 | bytes 11836416 | tf_op jit(solution)/shard_map/transpose(jvp())/reduce_sum | solution.py:32
  160.2 0.3 collective-permute-start.3
  160.5 0.6 fusion.47
  161.4 0.8 copy-done.7
  162.4 1.0 convolution_convert_fusion.1
  163.6 1.4 collective-permute-start.4
  165.0 0.4 convolution_convert_fusion.2
  165.4 2.1 collective-permute-done.4
  167.5 1.5 collective-permute-start.5
  169.0 2.4 collective-permute-done.5
  171.4 1.3 collective-permute-start.6
  172.7 2.0 multiply_convert_fusion
  174.9 0.3 collective-permute-done.6
  175.2 1.7 collective-permute-start.7
  177.0 0.9 maximum_select_fusion.1
  177.9 1.6 copy.33
  179.5 1.6 copy.34
  181.0 0.6 slice.127
  181.6 0.6 fusion.54
  182.2 103.0 %reduce-scatter.2.cloned.1.call-done = bf16[192,768]{1,0:T(8,128)(2,1)} async-done(((bf16[6144,768]{1,0:T(8,128)(2,1)}), bf16[192,768]{1,0:T(8,128)(2,1)}) %reduce-scatter.2.cloned.1.call-update) | async-done | bytes 294928 | tf_op jit(solution)/shard_map/reduce_scatter | solution.py:220
  285.3 1.0 convert_element_type.110
  286.3 0.7 slice_bitcast_fusion
  287.0 1.6 slice.126
  (100 shorter events, 2.0 us)
Async XLA Ops:
  7.2 9.0 %copy-start.5 = (bf16[1024,768]{1,0:T(8,128)(2,1)S(1)}, bf16[1024,768]{1,0:T(8,128)(2,1)}, u32[]{:S(2)}) copy-start(bf16[1024,768]{1,0:T(8,128)(2,1)} %param.21) | copy-start | bytes 4718596
  7.2 88.4 %all-gather.2.cloned.1.call-start = ((), (), s32[]{:S(2)}) async-start(), calls=%async_computation.1 | async-start | bytes 9732096 | tf_op jit(solution)/shard_map/all_gather | solution.py:160
  9.1 276.2 %reduce-scatter.2.cloned.1.call-start = ((), (), s32[]{:S(2)}) async-start(), calls=%async_computation.2 | async-start | bytes 9732096 | tf_op jit(solution)/shard_map/reduce_scatter | solution.py:220
  10.4 32.2 %collective-permute-start = (bf16[1,384]{1,0:T(2,128)(2,1)}, bf16[1,384]{1,0:T(2,128)(2,1)}, u32[]{:S(2)}, u32[]{:S(2)}) collective-permute-start(bf16[1,384]{1,0:T(2,128)(2,1)} %broadcast_in_dim.20), channel_id=1, source_target_pairs={{0,1},{1,0},{2,3},{3,2},{4,5},{5,4},{6,7},{7,6},{8,9},{9,8},{10,11... | collective-permute-start | bytes 2312 | tf_op jit(solution)/shard_map/ppermute | solution.py:163
  18.3 4.8 %copy-start.29 = (s32[2]{0:T(128)S(1)}, s32[2]{0:T(128)}, u32[]{:S(2)}) copy-start(s32[2]{0:T(128)} %param.12) | copy-start | bytes 28
  23.0 15.5 %copy-start.6 = (bf16[512,512]{1,0:T(8,128)(2,1)}, bf16[512,512]{1,0:T(8,128)(2,1)S(1)}, u32[]{:S(2)}) copy-start(bf16[512,512]{1,0:T(8,128)(2,1)S(1)} %get-tuple-element.75) | copy-start | bytes 1572868
  23.0 15.5 %copy-start.8 = (bf16[512,512]{1,0:T(8,128)(2,1)}, bf16[512,512]{1,0:T(8,128)(2,1)S(1)}, u32[]{:S(2)}) copy-start(bf16[512,512]{1,0:T(8,128)(2,1)S(1)} %get-tuple-element.76) | copy-start | bytes 1572868
  23.0 14.9 %copy-start.10 = (bf16[256,256]{1,0:T(8,128)(2,1)}, bf16[256,256]{1,0:T(8,128)(2,1)S(1)}, u32[]{:S(2)}) copy-start(bf16[256,256]{1,0:T(8,128)(2,1)S(1)} %slice.112) | copy-start | bytes 393220
  23.0 14.8 %copy-start.12 = (bf16[256,256]{1,0:T(8,128)(2,1)}, bf16[256,256]{1,0:T(8,128)(2,1)S(1)}, u32[]{:S(2)}) copy-start(bf16[256,256]{1,0:T(8,128)(2,1)S(1)} %slice.113) | copy-start | bytes 393220
  35.7 2.1 copy-start.1
  35.7 2.1 copy-start.3
  39.9 0.9 copy-start.14
  39.9 0.9 copy-start.21
  40.2 0.6 copy-start.22
  43.3 3.7 %collective-permute-start.1 = (bf16[2,384]{1,0:T(2,128)(2,1)S(1)}, bf16[2,384]{1,0:T(2,128)(2,1)S(1)}, u32[]{:S(2)}, u32[]{:S(2)}) collective-permute-start(bf16[2,384]{1,0:T(2,128)(2,1)S(1)} %pad_maximum_fusion.13), channel_id=1, source_target_pairs={{0,2},{1,3},{2,0},{3,1},{4,6},{5,7},{6,4},{7,5},{8,10},{9,11},{10,... | collective-permute-start | bytes 4616 | tf_op jit(solution)/shard_map/ppermute | solution.py:163
  47.0 8.1 %copy-start.28 = (bf16[2,384]{1,0:T(2,128)(2,1)}, bf16[2,384]{1,0:T(2,128)(2,1)S(1)}, u32[]{:S(2)}) copy-start(bf16[2,384]{1,0:T(2,128)(2,1)S(1)} %collective-permute-done.1) | copy-start | bytes 4612
  47.7 7.4 %collective-permute-start.2 = (bf16[4,384]{1,0:T(4,128)(2,1)S(1)}, bf16[4,384]{1,0:T(4,128)(2,1)}, u32[]{:S(2)}, u32[]{:S(2)}) collective-permute-start(bf16[4,384]{1,0:T(4,128)(2,1)S(1)} %pad_maximum_fusion.12), channel_id=1, source_target_pairs={{0,4},{1,5},{2,6},{3,7},{4,0},{5,1},{6,2},{7,3},{8,12},{9,13},{10,... | collective-permute-start | bytes 9224 | tf_op jit(solution)/shard_map/ppermute | solution.py:163
  111.4 3.1 %copy-start.15 = (f32[768]{0:T(1024)S(1)}, f32[768]{0:T(1024)}, u32[]{:S(2)}) copy-start(f32[768]{0:T(1024)} %param.17) | copy-start | bytes 9220
  114.5 2.4 copy-start.16
  114.5 2.4 copy-start.20
  116.8 2.7 copy-start
  116.9 2.7 copy-start.17
  117.6 4.6 %copy-start.18 = (f32[768]{0:T(1024)}, f32[768]{0:T(1024)S(1)}, u32[]{:S(2)}) copy-start(f32[768]{0:T(1024)S(1)} %get-tuple-element.61) | copy-start | bytes 9220
  117.6 4.6 %copy-start.19 = (f32[768]{0:T(1024)}, f32[768]{0:T(1024)S(1)}, u32[]{:S(2)}) copy-start(f32[768]{0:T(1024)S(1)} %get-tuple-element.62) | copy-start | bytes 9220
  119.6 2.6 copy-start.24
  155.5 4.7 %copy-start.26 = (f32[768]{0:T(1024)S(1)}, f32[768]{0:T(1024)}, u32[]{:S(2)}) copy-start(f32[768]{0:T(1024)} %get-tuple-element.32) | copy-start | bytes 9220
  155.5 4.7 %copy-start.25 = (f32[768]{0:T(1024)S(1)}, f32[768]{0:T(1024)}, u32[]{:S(2)}) copy-start(f32[768]{0:T(1024)} %get-tuple-element.37) | copy-start | bytes 9220
  155.5 5.0 %copy-start.23 = (f32[768]{0:T(1024)S(1)}, f32[768]{0:T(1024)}, u32[]{:S(2)}) copy-start(f32[768]{0:T(1024)} %copy-done.22) | copy-start | bytes 9220
  160.2 3.4 %collective-permute-start.3 = (f32[6912]{0:T(1024)S(1)}, f32[6912]{0:T(1024)S(1)}, u32[]{:S(2)}, u32[]{:S(2)}) collective-permute-start(f32[6912]{0:T(1024)S(1)} %constant_dynamic-update-slice_fusion), channel_id=1, source_target_pairs={{0,8},{8,0},{16,24},{24,16},{1,9},{9,1},{17,25},{25,17},{2,10},{10... | collective-permute-start | bytes 82952 | tf_op jit(solution)/shard_map/ppermute | solution.py:244
  161.1 1.1 copy-start.7
  161.1 1.3 copy-start.9
  163.4 1.6 copy-start.11
  163.4 1.6 copy-start.13
  163.5 9.2 %copy-start.2 = (bf16[768,768]{1,0:T(8,128)(2,1)S(1)}, bf16[768,768]{1,0:T(8,128)(2,1)}, u32[]{:S(2)}) copy-start(bf16[768,768]{1,0:T(8,128)(2,1)} %copy-done.1) | copy-start | bytes 3538948
  163.5 9.2 %copy-start.4 = (bf16[768,768]{1,0:T(8,128)(2,1)S(1)}, bf16[768,768]{1,0:T(8,128)(2,1)}, u32[]{:S(2)}) copy-start(bf16[768,768]{1,0:T(8,128)(2,1)} %copy-done.3) | copy-start | bytes 3538948
  163.6 3.9 %collective-permute-start.4 = (f32[6912]{0:T(1024)S(1)}, f32[6912]{0:T(1024)S(1)}, u32[]{:S(2)}, u32[]{:S(2)}) collective-permute-start(f32[6912]{0:T(1024)S(1)} %add.138), channel_id=1, source_target_pairs={{0,16},{8,24},{16,0},{24,8},{1,17},{9,25},{17,1},{25,9},{2,18},{10... | collective-permute-start | bytes 82952 | tf_op jit(solution)/shard_map/ppermute | solution.py:244
  167.5 3.9 %collective-permute-start.5 = (f32[6912]{0:T(1024)S(1)}, f32[6912]{0:T(1024)S(1)}, u32[]{:S(2)}, u32[]{:S(2)}) collective-permute-start(f32[6912]{0:T(1024)S(1)} %add.139), channel_id=1, source_target_pairs={{0,1},{1,0},{2,3},{3,2},{4,5},{5,4},{6,7},{7,6},{8,9},{9,8},{10,11... | collective-permute-start | bytes 82952 | tf_op jit(solution)/shard_map/ppermute | solution.py:244
  171.4 3.9 %collective-permute-start.6 = (f32[6912]{0:T(1024)S(1)}, f32[6912]{0:T(1024)S(1)}, u32[]{:S(2)}, u32[]{:S(2)}) collective-permute-start(f32[6912]{0:T(1024)S(1)} %add.140), channel_id=1, source_target_pairs={{0,2},{1,3},{2,0},{3,1},{4,6},{5,7},{6,4},{7,5},{8,10},{9,11},{10,... | collective-permute-start | bytes 82952 | tf_op jit(solution)/shard_map/ppermute | solution.py:244
  174.7 2.3 copy-start.27
  175.2 5.8 %collective-permute-start.7 = (f32[6912]{0:T(1024)S(1)}, f32[6912]{0:T(1024)S(1)}, u32[]{:S(2)}, u32[]{:S(2)}) collective-permute-start(f32[6912]{0:T(1024)S(1)} %add.141), channel_id=1, source_target_pairs={{0,4},{1,5},{2,6},{3,7},{4,0},{5,1},{6,2},{7,3},{8,12},{9,13},{10,... | collective-permute-start | bytes 82952 | tf_op jit(solution)/shard_map/ppermute | solution.py:244
Sparse Core Ops, SparseCore 0:
  11.5 84.0 all-gather.1
  150.5 134.7 reduce-scatter.1
